TPU v7x, 32 devices: a whole 2x2x4 slice. The times are simulated.
32 devices in a mesh: lat: 4 (over y, x), lon: 8 (over z, core).
Axes of the slice: x: 2, y: 2, z: 4, core: 2. Of those that a mesh axis runs over, the one named last changes fastest.
Arguments:
- fine_map: bfloat16 [4, 48, 256, 400], P(None, 'lat', 'lon'), may hold values from -26 to 26
- ocean_mask: int32 [4, 48, 256], P(None, 'lat', 'lon'), may hold values from 0 to 1
- out_grad: bfloat16 [4, 48, 256, 400], P(None, 'lat', 'lon'), may hold values from -6 to 6
- encode_depth: bfloat16 [7, 7, 400], replicated, may hold values from -0.875 to 0.875
- encode_gain: bfloat16 [400], replicated, may hold values from 0.099609375 to 1.8984375
- encode_shift: bfloat16 [400], replicated, may hold values from -3 to 3
- encode_up: bfloat16 [400, 1600], P('lat'), may hold values from -0.3125 to 0.3125
- encode_up_bias: bfloat16 [1600], replicated, may hold values from -3 to 3
- encode_down: bfloat16 [1600, 400], P('lat'), may hold values from -0.15625 to 0.15625
- encode_down_bias: bfloat16 [400], replicated, may hold values from -3 to 3
- widen_weight: bfloat16 [400, 800], P('lat'), may hold values from -0.3125 to 0.3125
- widen_bias: bfloat16 [800], replicated, may hold values from -3 to 3
- bottle_depth: bfloat16 [7, 7, 800], replicated, may hold values from -0.875 to 0.875
- bottle_gain: bfloat16 [800], replicated, may hold values from 0.099609375 to 1.8984375
- bottle_shift: bfloat16 [800], replicated, may hold values from -3 to 3
- bottle_up: bfloat16 [800, 3200], P('lat'), may hold values from -0.21875 to 0.21875
- bottle_up_bias: bfloat16 [3200], replicated, may hold values from -3 to 3
- bottle_down: bfloat16 [3200, 800], P('lat'), may hold values from -0.109375 to 0.109375
- bottle_down_bias: bfloat16 [800], replicated, may hold values from -3 to 3
- merge_weight: bfloat16 [1200, 400], P('lat'), may hold values from -0.1875 to 0.1875
- merge_bias: bfloat16 [400], replicated, may hold values from -3 to 3
- decode_depth: bfloat16 [7, 7, 400], replicated, may hold values from -0.875 to 0.875
- decode_gain: bfloat16 [400], replicated, may hold values from 0.099609375 to 1.8984375
- decode_shift: bfloat16 [400], replicated, may hold values from -3 to 3
- decode_up: bfloat16 [400, 1600], P('lat'), may hold values from -0.3125 to 0.3125
- decode_up_bias: bfloat16 [1600], replicated, may hold values from -3 to 3
- decode_down: bfloat16 [1600, 400], P('lat'), may hold values from -0.15625 to 0.15625
- decode_down_bias: bfloat16 [400], replicated, may hold values from -3 to 3
Outputs:
- result: bfloat16 [4, 48, 256, 400], P(None, 'lat', 'lon')
- fine_grad: bfloat16 [4, 48, 256, 400], P(None, 'lat', 'lon')
- encode_depth_grad: float32 [7, 7, 400], replicated
- encode_gain_grad: float32 [400], replicated
- encode_shift_grad: float32 [400], replicated
- encode_up_grad: float32 [400, 1600], replicated
- encode_up_bias_grad: float32 [1600], replicated
- encode_down_grad: float32 [1600, 400], replicated
- encode_down_bias_grad: float32 [400], replicated
- widen_weight_grad: float32 [400, 800], replicated
- widen_bias_grad: float32 [800], replicated
- bottle_depth_grad: float32 [7, 7, 800], replicated
- bottle_gain_grad: float32 [800], replicated
- bottle_shift_grad: float32 [800], replicated
- bottle_up_grad: float32 [800, 3200], replicated
- bottle_up_bias_grad: float32 [3200], replicated
- bottle_down_grad: float32 [3200, 800], replicated
- bottle_down_bias_grad: float32 [800], replicated
- merge_weight_grad: float32 [1200, 400], replicated
- merge_bias_grad: float32 [400], replicated
- decode_depth_grad: float32 [7, 7, 400], replicated
- decode_gain_grad: float32 [400], replicated
- decode_shift_grad: float32 [400], replicated
- decode_up_grad: float32 [400, 1600], replicated
- decode_up_bias_grad: float32 [1600], replicated
- decode_down_grad: float32 [1600, 400], replicated
- decode_down_bias_grad: float32 [400], replicated
All inputs are finite; a program needn't handle non-finite values.
Results may differ from a plain program's by a relative error of at most 0.018.
Values may be sent and summed in bfloat16 or wider, within the bound.
No kernel may reach another device: no remote copies, remote signals or barrier semaphores. Data moves between devices by JAX's collectives and lax.ppermute only.
A program may use at most 320 MiB of HBM per device.

v0:
```python
import math
import jax
import jax.numpy as jnp
from jax import lax
from jax.sharding import PartitionSpec as P

epsilon = 1e-05
both = ("lat", "lon")
bf16 = jnp.bfloat16
f32 = jnp.float32


def exchange_pairs(count, group, step):
    return [(i, i // group * group + (i % group ^ step)) for i in range(count)]


def to_dates(tiles):
    dates, count = (tiles.shape[0], lax.axis_size("lat"))
    own = lax.axis_index("lat") % dates
    pieces = [lax.dynamic_index_in_dim(tiles, own, 0, keepdims=False)]
    for step in range(1, dates):
        pieces.append(
            lax.ppermute(
                lax.dynamic_index_in_dim(tiles, own ^ step, 0, keepdims=False),
                "lat",
                exchange_pairs(count, dates, step),
            )
        )
    stacked = jnp.stack(pieces)
    ordered = [
        lax.dynamic_index_in_dim(stacked, own ^ tile, 0, keepdims=False) for tile in range(dates)
    ]
    return jnp.concatenate(ordered, axis=0)


def from_dates(band, dates):
    count = lax.axis_size("lat")
    own = lax.axis_index("lat") % dates
    tiles = band.reshape((dates, band.shape[0] // dates) + band.shape[1:])
    pieces = [lax.dynamic_index_in_dim(tiles, own, 0, keepdims=False)]
    for step in range(1, dates):
        pieces.append(
            lax.ppermute(
                lax.dynamic_index_in_dim(tiles, own ^ step, 0, keepdims=False),
                "lat",
                exchange_pairs(count, dates, step),
            )
        )
    stacked = jnp.stack(pieces)
    return jnp.stack(
        [lax.dynamic_index_in_dim(stacked, own ^ date, 0, keepdims=False) for date in range(dates)]
    )


def widen_map(source, dates):
    count = lax.axis_size("lon")
    forward = [(i, (i + 1) % count) for i in range(count)]
    backward = [(target, origin) for origin, target in forward]
    left = lax.ppermute(source[:, -3:], "lon", forward)
    right = lax.ppermute(source[:, :3], "lon", backward)
    wrapped = jnp.concatenate([left, source, right], axis=1)
    tiles = lax.axis_size("lat")
    if tiles == dates:
        return jnp.pad(wrapped, ((3, 3), (0, 0), (0, 0)))
    down = [(i, i + dates) for i in range(tiles - dates)]
    up = [(target, origin) for origin, target in down]
    above = lax.ppermute(wrapped[-3:], "lat", down)
    below = lax.ppermute(wrapped[:3], "lat", up)
    return jnp.concatenate([above, wrapped, below], axis=0)


def sum_all(local):
    count = lax.axis_size(both)
    copies = jnp.broadcast_to(local[None], (count,) + local.shape)
    return jnp.sum(lax.all_to_all(copies, both, 0, 0, tiled=False), axis=0)


def stencil(extended, kernel, height, breadth):
    taps = kernel.astype(f32)
    summed = jnp.zeros((height, breadth, extended.shape[2]), f32)
    for across in range(7):
        for column in range(7):
            summed = summed + taps[across, column] * extended[
                across : across + height, column : column + breadth, :
            ].astype(f32)
    return summed


def kernel_terms(extended, grad_mixed, height, breadth):
    upstream = grad_mixed.astype(f32)
    terms = []
    for across in range(7):
        for column in range(7):
            window = extended[across : across + height, column : column + breadth, :].astype(f32)
            terms.append(jnp.sum(window * upstream, axis=(0, 1)))
    return jnp.stack(terms)


def cross_rows(former, latter):
    return lax.dot_general(former, latter, (((0,), (0,)), ((), ())), preferred_element_type=f32)


def by_transpose(former, latter):
    return lax.dot_general(former, latter, (((1,), (1,)), ((), ())), preferred_element_type=f32)


def gelu_pair(hidden):
    phi = 0.5 * lax.erfc(hidden * -math.sqrt(0.5))
    density = jnp.exp(-0.5 * hidden * hidden) * (1.0 / math.sqrt(2.0 * math.pi))
    return (hidden * phi, phi + hidden * density)


def block_forward(source, params, sea, dates):
    kernel, gain, shift, up, up_bias, down, down_bias = params
    height, breadth, channels = source.shape
    extended = widen_map(source, dates)
    mixed = stencil(extended, kernel, height, breadth)
    masked = sea * mixed
    local = jnp.stack(
        [
            jnp.sum(masked, axis=(0, 1)),
            jnp.sum(masked * mixed, axis=(0, 1)),
            jnp.full((channels,), jnp.sum(sea)),
        ]
    )
    first, square, ocean = sum_all(local)
    ocean = ocean[0]
    mean = first / ocean
    factor = lax.rsqrt(square / ocean - mean * mean + epsilon)
    unit = (mixed - mean) * factor
    normed = (unit * gain.astype(f32) + shift.astype(f32)).astype(bf16).reshape(-1, channels)
    hidden = jnp.dot(normed, up, preferred_element_type=f32) + up_bias.astype(f32)
    active, slope = gelu_pair(hidden)
    active = active.astype(bf16)
    slope = slope.astype(bf16)
    branch = jnp.dot(active, down, preferred_element_type=f32) + down_bias.astype(f32)
    output = sea * (source.astype(f32) + branch.reshape(source.shape))
    return (output, (extended, mixed, mean, factor, ocean, normed, slope, active))


def block_backward(grad_output, params, sea, stored, dates):
    kernel, gain, shift, up, up_bias, down, down_bias = params
    extended, mixed, mean, factor, ocean, normed, slope, active = stored
    height, breadth, channels = mixed.shape
    grad_branch = (sea * grad_output).astype(bf16).reshape(-1, channels)
    grad_hidden = (by_transpose(grad_branch, down) * slope.astype(f32)).astype(bf16)
    grad_normed = by_transpose(grad_hidden, up).reshape(mixed.shape)
    unit = (mixed - mean) * factor
    local = jnp.stack([jnp.sum(grad_normed, axis=(0, 1)), jnp.sum(grad_normed * unit, axis=(0, 1))])
    grad_shift, grad_gain = sum_all(local)
    gain = gain.astype(f32)
    grad_mixed = factor * (
        gain * grad_normed - sea / ocean * (gain * grad_shift + unit * (gain * grad_gain))
    )
    grad_mixed = grad_mixed.astype(bf16)
    grad_extended = widen_map(grad_mixed, dates)
    grad_source = sea * grad_output + stencil(grad_extended, kernel[::-1, ::-1], height, breadth)
    grad_down = cross_rows(active, grad_branch)
    grad_down_bias = jnp.sum(grad_branch.astype(f32), axis=0)
    grad_up = cross_rows(normed, grad_hidden)
    grad_up_bias = jnp.sum(grad_hidden.astype(f32), axis=0)
    grad_kernel = kernel_terms(extended, grad_mixed, height, breadth)
    return (
        grad_source,
        (grad_kernel, grad_gain, grad_shift, grad_up, grad_up_bias, grad_down, grad_down_bias),
    )


def shards(
    fine_map,
    ocean_mask,
    out_grad,
    encode_depth,
    encode_gain,
    encode_shift,
    encode_up,
    encode_up_bias,
    encode_down,
    encode_down_bias,
    widen_weight,
    widen_bias,
    bottle_depth,
    bottle_gain,
    bottle_shift,
    bottle_up,
    bottle_up_bias,
    bottle_down,
    bottle_down_bias,
    merge_weight,
    merge_bias,
    decode_depth,
    decode_gain,
    decode_shift,
    decode_up,
    decode_up_bias,
    decode_down,
    decode_down_bias,
):
    (
        encode_up,
        encode_down,
        widen_weight,
        bottle_up,
        bottle_down,
        merge_weight,
        decode_up,
        decode_down,
    ) = (
        lax.all_gather(weight, "lat", axis=0, tiled=True)
        for weight in (
            encode_up,
            encode_down,
            widen_weight,
            bottle_up,
            bottle_down,
            merge_weight,
            decode_up,
            decode_down,
        )
    )
    dates = fine_map.shape[0]
    fine = to_dates(fine_map)
    sea_fine = to_dates(ocean_mask).astype(f32)[..., None]
    upstream = to_dates(out_grad)
    height, breadth, channels = fine.shape
    half_height, half_breadth = (height // 2, breadth // 2)
    wide = widen_weight.shape[1]
    sea_coarse = jnp.max(sea_fine.reshape(half_height, 2, half_breadth, 2, 1), axis=(1, 3))
    encode = (
        encode_depth,
        encode_gain,
        encode_shift,
        encode_up,
        encode_up_bias,
        encode_down,
        encode_down_bias,
    )
    bottle = (
        bottle_depth,
        bottle_gain,
        bottle_shift,
        bottle_up,
        bottle_up_bias,
        bottle_down,
        bottle_down_bias,
    )
    decode = (
        decode_depth,
        decode_gain,
        decode_shift,
        decode_up,
        decode_up_bias,
        decode_down,
        decode_down_bias,
    )
    merge_upper = merge_weight[:wide]
    merge_lower = merge_weight[wide:]
    encode_out, encode_stored = block_forward(fine, encode, sea_fine, dates)
    skip_map = encode_out.astype(bf16)
    skip_rows = skip_map.reshape(-1, channels)
    blocks = skip_map.reshape(half_height, 2, half_breadth, 2, channels).astype(f32)
    pooled = (jnp.sum(blocks, axis=(1, 3)) * 0.25).astype(bf16).reshape(-1, channels)
    coarse_in = jnp.dot(pooled, widen_weight, preferred_element_type=f32) + widen_bias.astype(f32)
    coarse_in = coarse_in.astype(bf16).reshape(half_height, half_breadth, wide)
    coarse_out, coarse_stored = block_forward(coarse_in, bottle, sea_coarse, dates)
    coarse_low = coarse_out.astype(bf16).reshape(-1, wide)
    upper = jnp.dot(coarse_low, merge_upper, preferred_element_type=f32)
    upper = upper.reshape(half_height, 1, half_breadth, 1, channels)
    lower = jnp.dot(skip_rows, merge_lower, preferred_element_type=f32)
    lower = lower.reshape(half_height, 2, half_breadth, 2, channels)
    merged = (lower + upper).reshape(height, breadth, channels) + merge_bias.astype(f32)
    decode_out, decode_stored = block_forward(merged.astype(bf16), decode, sea_fine, dates)
    result = from_dates(decode_out.astype(bf16), dates)
    grad_decode_in, decode_grads = block_backward(
        upstream.astype(f32), decode, sea_fine, decode_stored, dates
    )
    grad_merged = grad_decode_in.astype(bf16)
    grad_merged_rows = grad_merged.reshape(-1, channels)
    grad_block_sum = jnp.sum(
        grad_merged.astype(f32).reshape(half_height, 2, half_breadth, 2, channels), axis=(1, 3)
    ).reshape(-1, channels)
    grad_merge_bias = jnp.sum(grad_block_sum, axis=0)
    grad_block_low = grad_block_sum.astype(bf16)
    grad_block_rest = (grad_block_sum - grad_block_low.astype(f32)).astype(bf16)
    grad_merge_weight = jnp.concatenate(
        [
            cross_rows(coarse_low, grad_block_low) + cross_rows(coarse_low, grad_block_rest),
            cross_rows(skip_rows, grad_merged_rows),
        ],
        axis=0,
    )
    grad_coarse = (
        by_transpose(grad_block_low, merge_upper) + by_transpose(grad_block_rest, merge_upper)
    ).reshape(half_height, half_breadth, wide)
    grad_skip_direct = by_transpose(grad_merged_rows, merge_lower)
    grad_coarse_in, bottle_grads = block_backward(
        grad_coarse, bottle, sea_coarse, coarse_stored, dates
    )
    grad_wide = grad_coarse_in.astype(bf16).reshape(-1, wide)
    grad_widen_weight = cross_rows(pooled, grad_wide)
    grad_widen_bias = jnp.sum(grad_wide.astype(f32), axis=0)
    grad_pooled = (
        by_transpose(grad_wide, widen_weight).reshape(half_height, 1, half_breadth, 1, channels)
        * 0.25
    )
    grad_skip = grad_skip_direct.reshape(half_height, 2, half_breadth, 2, channels) + grad_pooled
    grad_fine, encode_grads = block_backward(
        grad_skip.reshape(height, breadth, channels), encode, sea_fine, encode_stored, dates
    )
    fine_grad = from_dates(grad_fine.astype(bf16), dates)

    def summed(parts):
        return [
            total.astype(f32) for total in lax.psum([part.astype(bf16) for part in parts], both)
        ]

    decode_up_sum, decode_down_sum, merge_sum = summed(
        [decode_grads[3], decode_grads[5], grad_merge_weight]
    )
    bottle_up_sum, bottle_down_sum, widen_sum = summed(
        [bottle_grads[3], bottle_grads[5], grad_widen_weight]
    )
    encode_up_sum, encode_down_sum = summed([encode_grads[3], encode_grads[5]])
    small_parts = [
        encode_grads[0],
        encode_grads[4],
        encode_grads[6],
        grad_widen_bias,
        bottle_grads[0],
        bottle_grads[4],
        bottle_grads[6],
        grad_merge_bias,
        decode_grads[0],
        decode_grads[4],
        decode_grads[6],
    ]
    small = lax.psum(small_parts, both)
    return (
        result,
        fine_grad,
        small[0].reshape(encode_depth.shape),
        encode_grads[1],
        encode_grads[2],
        encode_up_sum,
        small[1],
        encode_down_sum,
        small[2],
        widen_sum,
        small[3],
        small[4].reshape(bottle_depth.shape),
        bottle_grads[1],
        bottle_grads[2],
        bottle_up_sum,
        small[5],
        bottle_down_sum,
        small[6],
        merge_sum,
        small[7],
        small[8].reshape(decode_depth.shape),
        decode_grads[1],
        decode_grads[2],
        decode_up_sum,
        small[9],
        decode_down_sum,
        small[10],
    )


def solution(mesh):
    whole = P()
    rows = P("lat", None)
    tile = P(None, "lat", "lon", None)
    block = (whole, whole, whole, rows, whole, rows, whole)
    placed = (
        (tile, P(None, "lat", "lon"), tile) + block + (rows, whole) + block + (rows, whole) + block
    )
    return jax.shard_map(
        shards, mesh=mesh, in_specs=placed, out_specs=(tile, tile) + (whole,) * 25, check_vma=False
    )
```

profile of v0, /device:TPU:8, one launch (start us, length us, event | category | flops | bytes accessed | tf_op | source)
XLA Modules:
  0.0 1120.9 jit_solution(2642444557982647834)
XLA Ops:
  29.1 28.6 %all-gather.1 = bf16[4,300,400]{1,2,0:T(8,128)(2,1)S(1)} all-gather(bf16[1,300,400]{1,2,0:T(8,128)(2,1)S(1)} %bitcast.513), channel_id=1, replica_groups=mesh['lat'=4,'lon'=8] {'lat'}, dimensions={0}, use_global_device_ids=true | all-gather | bytes 1200000 | tf_op jit(solution)/shard_map/all_gather | solution.py:209
  59.1 11.9 %all-gather.2 = bf16[4,100,800]{2,1,0:T(8,128)(2,1)S(1)} all-gather(bf16[1,100,800]{2,1,0:T(8,128)(2,1)S(1)} %bitcast.516), channel_id=1, replica_groups=mesh['lat'=4,'lon'=8] {'lat'}, dimensions={0}, use_global_device_ids=true | all-gather | bytes 800000 | tf_op jit(solution)/shard_map/all_gather | solution.py:209
  105.8 28.1 %multiply_reduce_fusion.1 = (f32[400]{0:T(512)S(1)}, f32[400]{0:T(512)S(1)}, f32[48,32,400]{2,1,0:T(8,128)S(1)}) fusion(f32[48,32]{1,0:T(8,128)S(1)} %add_convert_fusion.9, bf16[54,38,400]{2,1,0:T(8,128)(2,1)S(1)} %select_maximum_fusion.6, f32[400]{0:T(512)S(1)} %bitcast.790, f32[400]{0:T(512)S(1)} %bitcast.789, f32[400]{0:T(512)S(1)} %bitcast.788, ...), kind=kLoop, calls=%fused_computation.236 | loop fusion | flops 94002400 | bytes 62756544 | tf_op jit(solution)/shard_map/reduce_sum | solution.py:121
  134.9 6.8 all-to-all-start
  148.5 5.2 reshape.448
  163.5 29.0 %multiply_convert_fusion.3 = (bf16[1536,1600]{0,1:T(8,128)(2,1)}, f32[1536,1600]{0,1:T(8,128)}, f32[1536,1600]{0,1:T(8,128)}) fusion(f32[1600]{0:T(1024)S(1)} %copy-done.382, bf16[1536,400]{1,0:T(8,128)(2,1)} %bitcast.500, bf16[400,1600]{1,0:T(8,128)(2,1)} %reshape.451), kind=kOutput, calls=%fused_computation.185 | convolution fusion | flops 2125824000 | bytes 27091200 | tf_op jit(solution)/shard_map/dot_general | solution.py:132
  192.6 7.3 multiply_convert_fusion.13
  203.3 6.1 reshape.426
  220.3 12.0 %multiply_reduce_fusion.4 = (f32[800]{0:T(1024)S(1)}, f32[800]{0:T(1024)S(1)}, f32[24,16,800]{2,1,0:T(8,128)S(1)}) fusion(f32[24,16]{1,0:T(8,128)S(1)} %copy.196, bf16[30,22,800]{2,1,0:T(8,128)(2,1)S(1)} %select_maximum_fusion.10, f32[800]{0:T(1024)S(1)} %copy-done.181, f32[800]{0:T(1024)S(1)} %copy-done.182, f32[800]{0:T(1024)S(1)} %copy-done.183, ...), kind=kLoop, calls=%fused_computation.643 | loop fusion | flops 51608000 | bytes 28043136 | tf_op jit(solution)/shard_map/reduce_sum | solution.py:121
  233.4 8.3 all-to-all-start.1
  256.0 16.4 %multiply_convert_fusion.4 = (bf16[384,3200]{1,0:T(8,128)(2,1)}, f32[384,3200]{1,0:T(8,128)}, f32[384,3200]{1,0:T(8,128)}) fusion(f32[3200]{0:T(1024)S(1)} %copy-done.219, bf16[384,800]{1,0:T(8,128)(2,1)S(1)} %bitcast.504, bf16[800,3200]{1,0:T(8,128)(2,1)} %all-gather.13.cloned.1.call-done), kind=kOutput, calls=%fused_computation.219 | convolution fusion | flops 2045952000 | bytes 18035200 | tf_op jit(solution)/shard_map/dot_general | solution.py:132
  272.5 6.5 fusion.440
  285.8 3.7 reshape.431
  302.6 30.9 %multiply_reduce_fusion = (f32[400]{0:T(512)S(1)}, f32[400]{0:T(512)S(1)}, f32[400]{0:T(512)}, f32[48,32,400]{2,1,0:T(8,128)}) fusion(f32[48,32]{1,0:T(8,128)S(1)} %copy-done.82, bf16[12,32,400]{2,1,0:T(8,128)(2,1)S(1)} %get-tuple-element.374, bf16[12,32,400]{2,1,0:T(8,128)(2,1)S(1)} %get-tuple-element.375, bf16[12,32,400]{2,1,0:T(8,128)(2,1)S(1)} %get-tuple-element.376, ...), kind=kLoop, calls=%fused_computation.234 | loop fusion | flops 110590800 | bytes 56844544 | tf_op jit(solution)/shard_map/reduce_sum | solution.py:121
  335.0 5.2 all-to-all-start.2
  350.8 5.3 reshape.430
  364.0 31.0 %multiply_convert_fusion.2 = (bf16[1536,1600]{0,1:T(8,128)(2,1)}, f32[1536,1600]{0,1:T(8,128)}, f32[1536,1600]{0,1:T(8,128)}) fusion(f32[1600]{0:T(1024)} %convert_element_type.1562, bf16[1536,400]{1,0:T(8,128)(2,1)S(1)} %bitcast.502, bf16[400,1600]{1,0:T(8,128)(2,1)S(1)} %reshape.457), kind=kOutput, calls=%fused_computation.172 | convolution fusion | flops 2125824000 | bytes 27091200 | tf_op jit(solution)/shard_map/dot_general | solution.py:132
  395.0 11.4 %convert_reduce_fusion = (f32[1600]{0:T(1024)}, bf16[1536,1600]{0,1:T(8,128)(2,1)S(1)}) fusion(f32[1536,1600]{0,1:T(8,128)} %get-tuple-element.328, f32[1536,1600]{0,1:T(8,128)} %get-tuple-element.609, bf16[1600,400]{1,0:T(8,128)(2,1)} %all-gather.17.cloned.1.call-done, f32[1536,400]{0,1:T(8,128)} %copy.210, f32[1536]{0:T(1024)S(1)} %copy-done.122), kind=kOutput, calls=%fused_computation.168 | convolution fusion | flops 1994340864 | bytes 28326144 | tf_op jit(solution)/shard_map/dot_general | solution.py:104
  406.4 4.4 fusion.488
  410.8 4.2 convolution_convert_fusion.3
  418.6 3.9 convolution_add_fusion.3
  433.5 5.8 all-to-all-start.3
  449.3 10.7 fusion.211
  461.2 9.0 fusion.212
  470.7 5.8 fusion.191
  488.6 28.8 %convert_reduce_fusion.8 = (f32[400]{0:T(512)}, bf16[48,32,400]{2,1,0:T(8,128)(2,1)S(1)}) fusion(bf16[54,38,400]{2,1,0:T(8,128)(2,1)S(1)} %select_maximum_fusion.2, f32[400]{0:T(512)S(1)} %bitcast.692, f32[400]{0:T(512)S(1)} %bitcast.691, f32[400]{0:T(512)S(1)} %bitcast.690, f32[400]{0:T(512)S(1)} %bitcast.689, f32[400]{0:T(512)S(1)} %bitcast.688, ...), kind=kLoop, calls=%fused_computation.909 | loop fusion | flops 108748400 | bytes 55612544 | tf_op jit(solution)/shard_map/reduce_sum | solution.py:282
  522.9 5.4 reduce_sum.1612
  534.2 9.6 convert_reduce_fusion.2
  543.8 5.2 convolution_convert_fusion.1
  556.2 7.8 all-to-all-start.4
  572.5 4.7 convolution_convert_fusion
  578.9 5.3 fusion.434
  585.0 3.9 fusion.435
  597.0 12.4 %convert_reduce_fusion.6 = (f32[800]{0:T(1024)}, bf16[24,16,800]{2,1,0:T(8,128)(2,1)S(1)}) fusion(bf16[30,22,800]{2,1,0:T(8,128)(2,1)S(1)} %select_maximum_fusion.8, f32[800]{0:T(1024)S(1)} %copy-done.146, f32[800]{0:T(1024)S(1)} %copy-done.147, f32[800]{0:T(1024)S(1)} %copy-done.148, f32[800]{0:T(1024)S(1)} %copy-done.149, f32[800]{0:T(1024)S(1)} %copy-done.150, ...), kind=kLoop, calls=%fused_computation.866 | loop fusion | flops 51916000 | bytes 28654336 | tf_op jit(solution)/shard_map/reduce_sum | solution.py:301
  621.9 10.6 convert_reduce_fusion.1
  632.6 3.8 fusion.490
  636.4 4.2 convolution_convert_fusion.5
  650.8 8.6 all-to-all-start.5
  666.6 43.7 %all-reduce.6 = (f32[1600]{0:T(1024)}, f32[400]{0:T(512)}, f32[800]{0:T(1024)}, f32[3200]{0:T(1024)}, f32[800]{0:T(1024)}, /*index=5*/f32[400]{0:T(512)}, f32[1600]{0:T(1024)}, f32[400]{0:T(512)}) all-reduce(f32[1600]{0:T(1024)S(1)} %get-tuple-element.617, ...), channel_id=1, replica_groups=mesh['lat'=4,'lon'=8] {'lat','lon'}, use_global_device_ids=true, to_apply=%region_75.76 | all-reduce | flops 9200 | bytes 73600 | tf_op jit(solution)/shard_map/psum | solution.py:337
  710.5 10.8 fusion.285
  722.0 9.0 fusion.286
  734.1 23.7 %add_convert_fusion = bf16[48,32,400]{2,1,0:T(8,128)(2,1)S(1)} fusion(f32[48,32,400]{2,1,0:T(8,128)S(1)} %copy-done.34, bf16[48,32,400]{2,1,0:T(8,128)(2,1)S(1)} %get-tuple-element.324, bf16[48,3,400]{2,1,0:T(4,128)(2,1)S(1)} %collective-permute-done.23, bf16[48,3,400]{2,1,0:T(4,128)(2,1)S(1)} %collective-permute-done.22, ...), kind=kLoop, calls=%fused_computation.590 | loop fusion | flops 102604800 | bytes 56839744 | tf_op jit(solution)/shard_map/convert_element_type | solution.py:310
  762.6 7.9 fusion.284
  773.6 13.1 %collective-permute-done.25 = bf16[12,32,400]{2,1,0:T(8,128)(2,1)S(1)} collective-permute-done((bf16[12,32,400]{2,1,0:T(8,128)(2,1)}, bf16[12,32,400]{2,1,0:T(8,128)(2,1)S(1)}, u32[]{:S(2)}, u32[]{:S(2)}) %collective-permute-start.25) | collective-permute-done | bytes 307232 | tf_op jit(solution)/shard_map/ppermute | solution.py:43
  790.4 182.3 %all-reduce.14.cloned.1.call-done = (bf16[400,1600]{1,0:T(8,128)(2,1)}, bf16[1600,400]{0,1:T(8,128)(2,1)}, bf16[400,800]{1,0:T(8,128)(2,1)}, bf16[800,3200]{1,0:...) async-done(((bf16[400,1600]{1,0:T(8,128)(2,1)}, bf16[1600,400]{0,1:T(8,128)(2,1)}, ...) | async-done | bytes 16960016 | tf_op jit(solution)/shard_map/psum | solution.py:314
  979.7 4.7 convert_element_type.1752
  984.4 4.7 convert_element_type.1755
  994.4 114.6 %all-reduce.12.cloned.1.call-done = (f32[7,7,400]{2,1,0:T(8,128)}, f32[7,7,800]{2,1,0:T(8,128)}, f32[7,7,400]{2,1,0:T(8,128)}) async-done(((f32[7,7,400]{2,1,0:T(8,128)}, f32[7,7,800]{2,1,0:T(8,128)}, f32[7,7,400]{2,1,0:T(8,128)}), (f32[7,7,400]{2,1,0:T(8,128)}, f32[7,7,800]{2,1,0:T(8,128)}, f32[7,7,400]{2,1,0:T(8,128)})) %all-reduce.12.cloned.1.call-update) | async-done | bytes 313616 | tf_op jit(solution)/shard_map/psum | solution.py:337
  (1167 shorter events, 277.7 us)
Async XLA Ops:
  7.2 153.8 %all-gather.19.cloned.1.call-start = ((), (), s32[]{:S(2)}) async-start(), calls=%async_computation.10 | async-start | bytes 1730560 | tf_op jit(solution)/shard_map/all_gather | solution.py:209
  8.0 184.6 %all-gather.11.cloned.1.call-start = ((), (), s32[]{:S(2)}) async-start(), calls=%async_computation.6 | async-start | bytes 2048000 | tf_op jit(solution)/shard_map/all_gather | solution.py:209
  8.7 247.3 %all-gather.13.cloned.1.call-start = ((), (), s32[]{:S(2)}) async-start(), calls=%async_computation.7 | async-start | bytes 6400000 | tf_op jit(solution)/shard_map/all_gather | solution.py:209
  9.5 263.0 %all-gather.15.cloned.1.call-start = ((), (), s32[]{:S(2)}) async-start(), calls=%async_computation.8 | async-start | bytes 7168000 | tf_op jit(solution)/shard_map/all_gather | solution.py:209
  10.1 336.5 %all-gather.21.cloned.1.call-start = ((), (), s32[]{:S(2)}) async-start(), calls=%async_computation.11 | async-start | bytes 1730560 | tf_op jit(solution)/shard_map/all_gather | solution.py:209
  10.6 384.3 %all-gather.17.cloned.1.call-start = ((), (), s32[]{:S(2)}) async-start(), calls=%async_computation.9 | async-start | bytes 2048000 | tf_op jit(solution)/shard_map/all_gather | solution.py:209
  12.0 62.0 %collective-permute-start.2 = (s32[12,32]{1,0:T(8,128)}, s32[12,32]{1,0:T(8,128)}, u32[]{:S(2)}, u32[]{:S(2)}) collective-permute-start(s32[12,32]{1,0:T(8,128)} %bitcast.479), channel_id=1, source_target_pairs={{0,24},{8,16},{16,8},{24,0},{1,25},{9,17},{17,9},{25,1},{2,26},{10... | collective-permute-start | bytes 4616 | tf_op jit(solution)/shard_map/ppermute | solution.py:23
  15.0 69.6 %collective-permute-start.1 = (s32[12,32]{1,0:T(8,128)}, s32[12,32]{1,0:T(8,128)}, u32[]{:S(2)}, u32[]{:S(2)}) collective-permute-start(s32[12,32]{1,0:T(8,128)} %bitcast.480), channel_id=1, source_target_pairs={{0,16},{8,24},{16,0},{24,8},{1,17},{9,25},{17,1},{25,9},{2,18},{10... | collective-permute-start | bytes 4616 | tf_op jit(solution)/shard_map/ppermute | solution.py:23
  16.7 73.9 %collective-permute-start.5 = (bf16[12,32,400]{2,1,0:T(8,128)(2,1)}, bf16[12,32,400]{2,1,0:T(8,128)(2,1)}, u32[]{:S(2)}, u32[]{:S(2)}) collective-permute-start(bf16[12,32,400]{2,1,0:T(8,128)(2,1)} %get-tuple-element.371), channel_id=1, source_target_pairs={{0,24},{8,16},{16,8},{24,0},{1,25},{9,17},{17,9},{25,1},{2,26},{10... | collective-permute-start | bytes 921608 | tf_op jit(solution)/shard_map/ppermute | solution.py:23
  18.2 73.1 %collective-permute-start.4 = (bf16[12,32,400]{2,1,0:T(8,128)(2,1)}, bf16[12,32,400]{2,1,0:T(8,128)(2,1)}, u32[]{:S(2)}, u32[]{:S(2)}) collective-permute-start(bf16[12,32,400]{2,1,0:T(8,128)(2,1)} %get-tuple-element.372), channel_id=1, source_target_pairs={{0,16},{8,24},{16,0},{24,8},{1,17},{9,25},{17,1},{25,9},{2,18},{10... | collective-permute-start | bytes 921608 | tf_op jit(solution)/shard_map/ppermute | solution.py:23
  18.7 72.6 %collective-permute-start.3 = (bf16[12,32,400]{2,1,0:T(8,128)(2,1)}, bf16[12,32,400]{2,1,0:T(8,128)(2,1)}, u32[]{:S(2)}, u32[]{:S(2)}) collective-permute-start(bf16[12,32,400]{2,1,0:T(8,128)(2,1)} %get-tuple-element.370), channel_id=1, source_target_pairs={{0,8},{8,0},{16,24},{24,16},{1,9},{9,1},{17,25},{25,17},{2,10},{10... | collective-permute-start | bytes 921608 | tf_op jit(solution)/shard_map/ppermute | solution.py:23
  28.2 47.7 %copy-start.403 = (bf16[400]{0:T(512)(128)(2,1)S(1)}, bf16[400]{0:T(512)(128)(2,1)}, u32[]{:S(2)}) copy-start(bf16[400]{0:T(512)(128)(2,1)} %param.33) | copy-start | bytes 2404
  28.3 48.3 %copy-start.391 = (bf16[400]{0:T(512)(128)(2,1)S(1)}, bf16[400]{0:T(512)(128)(2,1)}, u32[]{:S(2)}) copy-start(bf16[400]{0:T(512)(128)(2,1)} %param.32) | copy-start | bytes 2404
  28.3 48.9 %copy-start.379 = (bf16[3200]{0:T(1024)(128)(2,1)S(1)}, bf16[3200]{0:T(1024)(128)(2,1)}, u32[]{:S(2)}) copy-start(bf16[3200]{0:T(1024)(128)(2,1)} %param.44) | copy-start | bytes 19204
  28.3 49.5 %copy-start.395 = (bf16[800]{0:T(1024)(128)(2,1)S(1)}, bf16[800]{0:T(1024)(128)(2,1)}, u32[]{:S(2)}) copy-start(bf16[800]{0:T(1024)(128)(2,1)} %param.39) | copy-start | bytes 4804
  28.3 50.1 %copy-start.396 = (bf16[800]{0:T(1024)(128)(2,1)S(1)}, bf16[800]{0:T(1024)(128)(2,1)}, u32[]{:S(2)}) copy-start(bf16[800]{0:T(1024)(128)(2,1)} %param.42) | copy-start | bytes 4804
  28.3 50.6 %copy-start.380 = (bf16[800]{0:T(1024)(128)(2,1)S(1)}, bf16[800]{0:T(1024)(128)(2,1)}, u32[]{:S(2)}) copy-start(bf16[800]{0:T(1024)(128)(2,1)} %param.41) | copy-start | bytes 4804
  28.3 51.2 %copy-start.397 = (bf16[800]{0:T(1024)(128)(2,1)S(1)}, bf16[800]{0:T(1024)(128)(2,1)}, u32[]{:S(2)}) copy-start(bf16[800]{0:T(1024)(128)(2,1)} %param.46) | copy-start | bytes 4804
  74.0 11.5 %collective-permute-start = (s32[12,32]{1,0:T(8,128)S(1)}, s32[12,32]{1,0:T(8,128)S(1)}, u32[]{:S(2)}, u32[]{:S(2)}) collective-permute-start(s32[12,32]{1,0:T(8,128)S(1)} %bitcast.835), channel_id=1, source_target_pairs={{0,8},{8,0},{16,24},{24,16},{1,9},{9,1},{17,25},{25,17},{2,10},{10... | collective-permute-start | bytes 4616 | tf_op jit(solution)/shard_map/ppermute | solution.py:23
  84.6 162.4 %collective-permute-start.17 = (bf16[12,32,400]{2,1,0:T(8,128)(2,1)}, bf16[12,32,400]{2,1,0:T(8,128)(2,1)}, u32[]{:S(2)}, u32[]{:S(2)}) collective-permute-start(bf16[12,32,400]{2,1,0:T(8,128)(2,1)} %get-tuple-element.379), channel_id=1, source_target_pairs={{0,24},{8,16},{16,8},{24,0},{1,25},{9,17},{17,9},{25,1},{2,26},{10... | collective-permute-start | bytes 921608 | tf_op jit(solution)/shard_map/ppermute | solution.py:23
  85.5 161.6 %collective-permute-start.16 = (bf16[12,32,400]{2,1,0:T(8,128)(2,1)}, bf16[12,32,400]{2,1,0:T(8,128)(2,1)}, u32[]{:S(2)}, u32[]{:S(2)}) collective-permute-start(bf16[12,32,400]{2,1,0:T(8,128)(2,1)} %get-tuple-element.380), channel_id=1, source_target_pairs={{0,16},{8,24},{16,0},{24,8},{1,17},{9,25},{17,1},{25,9},{2,18},{10... | collective-permute-start | bytes 921608 | tf_op jit(solution)/shard_map/ppermute | solution.py:23
  90.6 156.5 %collective-permute-start.15 = (bf16[12,32,400]{2,1,0:T(8,128)(2,1)}, bf16[12,32,400]{2,1,0:T(8,128)(2,1)}, u32[]{:S(2)}, u32[]{:S(2)}) collective-permute-start(bf16[12,32,400]{2,1,0:T(8,128)(2,1)} %get-tuple-element.378), channel_id=1, source_target_pairs={{0,8},{8,0},{16,24},{24,16},{1,9},{9,1},{17,25},{25,17},{2,10},{10... | collective-permute-start | bytes 921608 | tf_op jit(solution)/shard_map/ppermute | solution.py:23
  95.4 5.3 collective-permute-start.7
  95.4 6.6 collective-permute-start.6
  134.9 22.1 %all-to-all-start = ((f32[32,3,400]{2,1,0:T(4,128)}), f32[32,3,400]{2,1,0:T(4,128)}, u32[]{:S(2)}, u32[]{:S(2)}) async-start(f32[32,3,400]{2,1,0:T(4,128)} %broadcast_in_dim.12), calls=%async_computation | async-start | bytes 524288 | tf_op jit(solution)/shard_map/all_to_all | solution.py:75
  214.3 3.6 collective-permute-start.9
  214.4 4.9 collective-permute-start.8
  233.4 21.0 %all-to-all-start.1 = ((f32[32,3,800]{2,1,0:T(4,128)}), f32[32,3,800]{2,1,0:T(4,128)S(1)}, u32[]{:S(2)}, u32[]{:S(2)}) async-start(f32[32,3,800]{2,1,0:T(4,128)} %broadcast_in_dim.13), calls=%async_computation.1 | async-start | bytes 917504 | tf_op jit(solution)/shard_map/all_to_all | solution.py:75
  292.2 5.4 collective-permute-start.11
  294.8 6.2 collective-permute-start.10
  335.0 21.2 %all-to-all-start.2 = ((f32[32,3,400]{2,1,0:T(4,128)}), f32[32,3,400]{2,1,0:T(4,128)}, u32[]{:S(2)}, u32[]{:S(2)}) async-start(f32[32,3,400]{2,1,0:T(4,128)} %broadcast_in_dim.14), calls=%async_computation.2 | async-start | bytes 524288 | tf_op jit(solution)/shard_map/all_to_all | solution.py:75
  433.5 15.7 %all-to-all-start.3 = ((f32[32,2,400]{2,1,0:T(2,128)}), f32[32,2,400]{2,1,0:T(2,128)S(1)}, u32[]{:S(2)}, u32[]{:S(2)}) async-start(f32[32,2,400]{2,1,0:T(2,128)} %broadcast_in_dim.15), calls=%async_computation.3 | async-start | bytes 262144 | tf_op jit(solution)/shard_map/all_to_all | solution.py:75
  443.8 40.0 %collective-permute-start.14 = (bf16[12,32,400]{2,1,0:T(8,128)(2,1)}, bf16[12,32,400]{2,1,0:T(8,128)(2,1)S(1)}, u32[]{:S(2)}, u32[]{:S(2)}) collective-permute-start(bf16[12,32,400]{2,1,0:T(8,128)(2,1)} %get-tuple-element.354), channel_id=1, source_target_pairs={{0,24},{8,16},{16,8},{24,0},{1,25},{9,17},{17,9},{25,1},{2,26},{10... | collective-permute-start | bytes 921608 | tf_op jit(solution)/shard_map/ppermute | solution.py:43
  446.1 37.7 %collective-permute-start.13 = (bf16[12,32,400]{2,1,0:T(8,128)(2,1)}, bf16[12,32,400]{2,1,0:T(8,128)(2,1)}, u32[]{:S(2)}, u32[]{:S(2)}) collective-permute-start(bf16[12,32,400]{2,1,0:T(8,128)(2,1)} %get-tuple-element.355), channel_id=1, source_target_pairs={{0,16},{8,24},{16,0},{24,8},{1,17},{9,25},{17,1},{25,9},{2,18},{10... | collective-permute-start | bytes 921608 | tf_op jit(solution)/shard_map/ppermute | solution.py:43
  446.7 37.1 %collective-permute-start.12 = (bf16[12,32,400]{2,1,0:T(8,128)(2,1)}, bf16[12,32,400]{2,1,0:T(8,128)(2,1)}, u32[]{:S(2)}, u32[]{:S(2)}) collective-permute-start(bf16[12,32,400]{2,1,0:T(8,128)(2,1)} %get-tuple-element.356), channel_id=1, source_target_pairs={{0,8},{8,0},{16,24},{24,16},{1,9},{9,1},{17,25},{25,17},{2,10},{10... | collective-permute-start | bytes 921608 | tf_op jit(solution)/shard_map/ppermute | solution.py:43
  470.2 16.9 %collective-permute-start.19 = (bf16[48,3,400]{2,1,0:T(4,128)(2,1)}, bf16[48,3,400]{2,1,0:T(4,128)(2,1)S(1)}, u32[]{:S(2)}, u32[]{:S(2)}) collective-permute-start(bf16[48,3,400]{2,1,0:T(4,128)(2,1)} %get-tuple-element.348), channel_id=1, source_target_pairs={{1,0},{2,1},{3,2},{4,3},{5,4},{6,5},{7,6},{0,7},{9,8},{10,9},{11,1... | collective-permute-start | bytes 345608 | tf_op jit(solution)/shard_map/ppermute | solution.py:60
  470.2 16.9 %collective-permute-start.18 = (bf16[48,3,400]{2,1,0:T(4,128)(2,1)}, bf16[48,3,400]{2,1,0:T(4,128)(2,1)S(1)}, u32[]{:S(2)}, u32[]{:S(2)}) collective-permute-start(bf16[48,3,400]{2,1,0:T(4,128)(2,1)} %get-tuple-element.347), channel_id=1, source_target_pairs={{0,1},{1,2},{2,3},{3,4},{4,5},{5,6},{6,7},{7,0},{8,9},{9,10},{10,1... | collective-permute-start | bytes 345608 | tf_op jit(solution)/shard_map/ppermute | solution.py:59
  556.2 21.0 %all-to-all-start.4 = ((f32[32,2,800]{2,1,0:T(2,128)}), f32[32,2,800]{2,1,0:T(2,128)}, u32[]{:S(2)}, u32[]{:S(2)}) async-start(f32[32,2,800]{2,1,0:T(2,128)} %broadcast_in_dim.16), calls=%async_computation.4 | async-start | bytes 458752 | tf_op jit(solution)/shard_map/all_to_all | solution.py:75
  588.9 6.2 collective-permute-start.21
  589.1 6.0 collective-permute-start.20
  650.8 59.5 %all-to-all-start.5 = ((f32[32,2,400]{2,1,0:T(2,128)}), f32[32,2,400]{2,1,0:T(2,128)S(1)}, u32[]{:S(2)}, u32[]{:S(2)}) async-start(f32[32,2,400]{2,1,0:T(2,128)} %broadcast_in_dim.17), calls=%async_computation.5 | async-start | bytes 262144 | tf_op jit(solution)/shard_map/all_to_all | solution.py:75
  659.5 313.2 %all-reduce.14.cloned.1.call-start = ((), (), s32[]{:S(2)}) async-start(), calls=%async_computation.13 | async-start | bytes 34611200 | tf_op jit(solution)/shard_map/psum | solution.py:314
  665.9 443.1 %all-reduce.12.cloned.1.call-start = ((), (), s32[]{:S(2)}) async-start(), calls=%async_computation.12 | async-start | bytes 860160 | tf_op jit(solution)/shard_map/psum | solution.py:337
  721.5 9.9 collective-permute-start.23
  721.5 11.1 collective-permute-start.22
  758.8 14.7 %collective-permute-start.26 = (bf16[12,32,400]{2,1,0:T(8,128)(2,1)}, bf16[12,32,400]{2,1,0:T(8,128)(2,1)S(1)}, u32[]{:S(2)}, u32[]{:S(2)}) collective-permute-start(bf16[12,32,400]{2,1,0:T(8,128)(2,1)} %get-tuple-element.342), channel_id=1, source_target_pairs={{0,24},{8,16},{16,8},{24,0},{1,25},{9,17},{17,9},{25,1},{2,26},{10... | collective-permute-start | bytes 921608 | tf_op jit(solution)/shard_map/ppermute | solution.py:43
  761.3 25.4 %collective-permute-start.25 = (bf16[12,32,400]{2,1,0:T(8,128)(2,1)}, bf16[12,32,400]{2,1,0:T(8,128)(2,1)S(1)}, u32[]{:S(2)}, u32[]{:S(2)}) collective-permute-start(bf16[12,32,400]{2,1,0:T(8,128)(2,1)} %get-tuple-element.343), channel_id=1, source_target_pairs={{0,16},{8,24},{16,0},{24,8},{1,17},{9,25},{17,1},{25,9},{2,18},{10... | collective-permute-start | bytes 921608 | tf_op jit(solution)/shard_map/ppermute | solution.py:43
  762.6 25.0 %collective-permute-start.24 = (bf16[12,32,400]{2,1,0:T(8,128)(2,1)}, bf16[12,32,400]{2,1,0:T(8,128)(2,1)}, u32[]{:S(2)}, u32[]{:S(2)}) collective-permute-start(bf16[12,32,400]{2,1,0:T(8,128)(2,1)} %get-tuple-element.344), channel_id=1, source_target_pairs={{0,8},{8,0},{16,24},{24,16},{1,9},{9,1},{17,25},{25,17},{2,10},{10... | collective-permute-start | bytes 921608 | tf_op jit(solution)/shard_map/ppermute | solution.py:43
  (409 other events, 3263.0 us)
Sparse Core Ops, SparseCore 0:
  9.9 47.4 all-gather.18
  59.3 45.4 all-gather.10
  106.6 63.3 all-gather.12
  171.7 65.5 all-gather.14
  238.9 30.6 all-gather.20
  271.3 31.5 all-gather.16
  668.5 304.1 all-reduce.13
  980.1 128.8 all-reduce.11
where the time goes:
time: 1130 us; the launch traced here: 1120 us
  waiting for transfers between devices  325 us (29%)
  other arithmetic  301 us (27%)
  matrix products  180 us (16%)
  local copies, waits for them, and re-layouts  144 us (13%)
  blocking collectives  84.2 us (7%)
  starting transfers between devices  66.2 us (6%)
  between operations  20.9 us (2%)
    psum x1, waiting for transfers between devices, summed(): lax.psum([part.astype(bf16) for part in parts], both)  182 us
    psum x1, waiting for transfers between devices, shards(): small = lax.psum(small_parts, both)  115 us
    dot_general x3, matrix products, block_forward(): jnp.dot(normed, up, preferred_element_type=f32) + up_bias.astype(f32)  76.4 us
    reduce_sum x3, other arithmetic, block_forward(): jnp.sum(masked, axis=(0, 1))  71 us
    reduce_sum x11, other arithmetic, kernel_terms(): terms.append(jnp.sum(window * upstream, axis=(0, 1)))  69.6 us
    dot_general x10, matrix products, by_transpose(): lax.dot_general(former, latter, (((1,), (1,)), ((), ())), preferred_eleme...  48.7 us
    psum x1, blocking collectives, shards(): small = lax.psum(small_parts, both)  43.7 us
    all_to_all x6, starting transfers between devices, sum_all(): return jnp.sum(lax.all_to_all(copies, both, 0, 0, tiled=False), axis=0)  42.6 us
  transfers between devices with their start and end apart: 41, of which 10 were waited for; matrix products, arithmetic and copies ran while one was open for 39% of the time, Pallas kernels for 0%

commit v1 on v0

--- a/solution.py
+++ b/solution.py
@@ -311,7 +311,8 @@
 
     def summed(parts):
         return [
-            total.astype(f32) for total in lax.psum([part.astype(bf16) for part in parts], both)
+            total.astype(f32)
+            for total in lax.psum(lax.psum([part.astype(bf16) for part in parts], "lon"), "lat")
         ]
 
     decode_up_sum, decode_down_sum, merge_sum = summed(

time: 1130 us -> 1470 us (1.30)
  waiting for transfers between devices: 325 us -> 628 us
  local copies, waits for them, and re-layouts: 144 us -> 160 us
    psum x1 -> x2, waiting for transfers between devices: 182 us -> 473 us  [the longest x1 295 us: summed(): lax.psum([part.astype(bf16) for part in parts], 'lon')]
  transfers between devices with their start and end apart: 41 -> 42, of which waited for: 10 -> 11; matrix products, arithmetic and copies ran while one was open for 39% -> 33% of each run, Pallas kernels for 0% -> 0%
where the time goes in v1:
time: 1470 us; the launch traced here: 1460 us
  waiting for transfers between devices  628 us (43%)
  other arithmetic  310 us (21%)
  matrix products  194 us (13%)
  local copies, waits for them, and re-layouts  160 us (11%)
  blocking collectives  83.5 us (6%)
  starting transfers between devices  63.2 us (4%)
  between operations  20.3 us (1%)
    psum x1, waiting for transfers between devices, summed(): lax.psum([part.astype(bf16) for part in parts], 'lon')  295 us
    psum x1, waiting for transfers between devices, summed(): lax.psum(lax.psum([part.astype(bf16) for part in parts], 'lon'), 'lat')  178 us
    psum x1, waiting for transfers between devices, shards(): small = lax.psum(small_parts, both)  116 us
    dot_general x3, matrix products, block_forward(): jnp.dot(normed, up, preferred_element_type=f32) + up_bias.astype(f32)  76.8 us
    reduce_sum x11, other arithmetic, kernel_terms(): terms.append(jnp.sum(window * upstream, axis=(0, 1)))  72 us
    reduce_sum x3, other arithmetic, block_forward(): jnp.sum(masked, axis=(0, 1))  71.9 us
    dot_general x10, matrix products, by_transpose(): lax.dot_general(former, latter, (((1,), (1,)), ((), ())), preferred_eleme...  48.6 us
    dot_general x10, matrix products, cross_rows(): lax.dot_general(former, latter, (((0,), (0,)), ((), ())), preferred_eleme...  43.2 us
  transfers between devices with their start and end apart: 42, of which 11 were waited for; matrix products, arithmetic and copies ran while one was open for 33% of the time, Pallas kernels for 0%

profile of v1, /device:TPU:8, one launch (start us, length us, event | category | flops | bytes accessed | tf_op | source)
XLA Modules:
  0.0 1459.3 jit_solution(18407899613325765355)
XLA Ops:
  26.4 29.5 %all-gather.1 = bf16[4,300,400]{1,2,0:T(8,128)(2,1)S(1)} all-gather(bf16[1,300,400]{1,2,0:T(8,128)(2,1)S(1)} %bitcast.514), channel_id=1, replica_groups=mesh['lat'=4,'lon'=8] {'lat'}, dimensions={0}, use_global_device_ids=true | all-gather | bytes 1200000 | tf_op jit(solution)/shard_map/all_gather | solution.py:209
  57.4 12.0 all-gather.2
  102.5 28.9 %multiply_reduce_fusion.1 = (f32[400]{0:T(512)S(1)}, f32[400]{0:T(512)S(1)}, f32[48,32,400]{2,1,0:T(8,128)}) fusion(f32[48,32]{1,0:T(8,128)S(1)} %add_convert_fusion.9, bf16[54,38,400]{2,1,0:T(8,128)(2,1)S(1)} %select_maximum_fusion.6, f32[400]{0:T(512)S(1)} %bitcast.791, f32[400]{0:T(512)S(1)} %bitcast.790, f32[400]{0:T(512)S(1)} %bitcast.789, ...), kind=kLoop, calls=%fused_computation.236 | loop fusion | flops 94002400 | bytes 62756544 | tf_op jit(solution)/shard_map/reduce_sum | solution.py:121
  132.3 5.9 all-to-all-start
  141.8 5.2 reshape.448
  156.3 30.1 %multiply_convert_fusion.3 = (bf16[1536,1600]{0,1:T(8,128)(2,1)}, f32[1536,1600]{0,1:T(8,128)}, f32[1536,1600]{0,1:T(8,128)}) fusion(f32[1600]{0:T(1024)S(1)} %copy-done.374, bf16[1536,400]{1,0:T(8,128)(2,1)S(1)} %bitcast.502, bf16[400,1600]{1,0:T(8,128)(2,1)S(1)} %reshape.451), kind=kOutput, calls=%fused_computation.185 | convolution fusion | flops 2125824000 | bytes 27091200 | tf_op jit(solution)/shard_map/dot_general | solution.py:132
  186.4 8.0 multiply_convert_fusion.13
  197.9 5.2 reshape.426
  216.9 12.0 multiply_reduce_fusion.4
  229.9 8.0 all-to-all-start.1
  252.3 16.6 %multiply_convert_fusion.4 = (bf16[384,3200]{1,0:T(8,128)(2,1)}, f32[384,3200]{1,0:T(8,128)}, f32[384,3200]{1,0:T(8,128)}) fusion(f32[3200]{0:T(1024)S(1)} %copy-done.192, bf16[384,800]{1,0:T(8,128)(2,1)S(1)} %bitcast.506, bf16[800,3200]{1,0:T(8,128)(2,1)} %all-gather.13.cloned.1.call-done), kind=kOutput, calls=%fused_computation.219 | convolution fusion | flops 2045952000 | bytes 18035200 | tf_op jit(solution)/shard_map/dot_general | solution.py:132
  269.0 6.5 fusion.440
  283.4 5.3 reshape.431
  301.4 30.9 %multiply_reduce_fusion = (f32[400]{0:T(512)S(1)}, f32[400]{0:T(512)S(1)}, f32[400]{0:T(512)}, f32[48,32,400]{2,1,0:T(8,128)}) fusion(f32[48,32]{1,0:T(8,128)S(1)} %copy-done.74, bf16[12,32,400]{2,1,0:T(8,128)(2,1)S(1)} %get-tuple-element.382, bf16[12,32,400]{2,1,0:T(8,128)(2,1)S(1)} %get-tuple-element.383, bf16[12,32,400]{2,1,0:T(8,128)(2,1)S(1)} %get-tuple-element.384, ...), kind=kLoop, calls=%fused_computation.234 | loop fusion | flops 110590800 | bytes 56844544 | tf_op jit(solution)/shard_map/reduce_sum | solution.py:121
  354.9 30.1 %multiply_convert_fusion.2 = (bf16[1536,1600]{0,1:T(8,128)(2,1)}, f32[1536,1600]{0,1:T(8,128)}, f32[1536,1600]{0,1:T(8,128)}) fusion(f32[1600]{0:T(1024)S(1)} %copy-done.373, bf16[1536,400]{1,0:T(8,128)(2,1)S(1)} %bitcast.504, bf16[400,1600]{1,0:T(8,128)(2,1)S(1)} %copy-done.70), kind=kOutput, calls=%fused_computation.172 | convolution fusion | flops 2125824000 | bytes 27091200 | tf_op jit(solution)/shard_map/dot_general | solution.py:132
  385.0 11.2 convert_reduce_fusion
  407.5 6.0 all-to-all-start.3
  413.6 6.7 convolution_convert_fusion.2
  423.3 11.5 fusion.211
  435.6 6.5 convolution_convert_fusion.3
  444.0 29.3 %convert_reduce_fusion.8 = (f32[400]{0:T(512)}, bf16[48,32,400]{2,1,0:T(8,128)(2,1)}) fusion(bf16[54,38,400]{2,1,0:T(8,128)(2,1)S(1)} %select_maximum_fusion.2, f32[400]{0:T(512)S(1)} %bitcast.693, f32[400]{0:T(512)S(1)} %bitcast.692, f32[400]{0:T(512)S(1)} %bitcast.691, f32[400]{0:T(512)S(1)} %bitcast.690, f32[400]{0:T(512)S(1)} %bitcast.689, ...), kind=kLoop, calls=%fused_computation.909 | loop fusion | flops 108748400 | bytes 55612544 | tf_op jit(solution)/shard_map/reduce_sum | solution.py:282
  473.4 5.1 reshape.435
  478.5 5.3 reduce_sum.1612
  489.9 9.6 convert_reduce_fusion.2
  499.4 5.3 convolution_convert_fusion.1
  514.3 8.7 all-to-all-start.4
  536.1 6.2 fusion.434
  554.2 14.0 convert_reduce_fusion.6
  577.4 5.3 reshape.440
  586.1 6.8 convolution_convert_fusion.4
  592.9 9.9 convert_reduce_fusion.1
  618.1 5.6 reshape.430
  623.8 6.9 convolution_add_fusion.3
  642.3 5.5 fusion.191
  647.7 9.6 fusion.212
  661.0 5.2 stack.772
  666.9 295.0 %all-reduce.16.cloned.1.call-done = (bf16[400,1600]{1,0:T(8,128)(2,1)}, bf16[1600,400]{0,1:T(8,128)(2,1)}, bf16[400,800]{1,0:T(8,128)(2,1)}, bf16[800,3200]{1,0:...) async-done(((bf16[400,1600]{1,0:T(8,128)(2,1)}, bf16[1600,400]{0,1:T(8,128)(2,1)}, ...) | async-done | bytes 16960016 | tf_op jit(solution)/shard_map/psum | solution.py:315
  992.4 5.5 reshape.439
  997.9 42.0 %all-reduce.6 = (f32[1600]{0:T(1024)}, f32[400]{0:T(512)}, f32[800]{0:T(1024)}, f32[3200]{0:T(1024)}, f32[800]{0:T(1024)}, /*index=5*/f32[400]{0:T(512)}, f32[1600]{0:T(1024)}, f32[400]{0:T(512)}) all-reduce(f32[1600]{0:T(1024)S(1)} %copy-done.126, f32[400]{0:T(512)S(1)} %copy-done.392, ...), channel_id=1, replica_groups=mesh['lat'=4,'lon'=8] {'lat','lon'}, use_global_device_ids=true, to_apply=%region_76.77 | all-reduce | flops 9200 | bytes 73600 | tf_op jit(solution)/shard_map/psum | solution.py:338
  1041.0 10.7 fusion.285
  1052.5 9.8 fusion.286
  1064.5 23.8 %add_convert_fusion = bf16[48,32,400]{2,1,0:T(8,128)(2,1)S(1)} fusion(f32[48,32,400]{2,1,0:T(8,128)S(1)} %copy-done.29, bf16[48,32,400]{2,1,0:T(8,128)(2,1)S(1)} %get-tuple-element.332, bf16[48,3,400]{2,1,0:T(4,128)(2,1)S(1)} %collective-permute-done.23, bf16[48,3,400]{2,1,0:T(4,128)(2,1)S(1)} %collective-permute-done.22, ...), kind=kLoop, calls=%fused_computation.590 | loop fusion | flops 102604800 | bytes 56839744 | tf_op jit(solution)/shard_map/convert_element_type | solution.py:310
  1093.4 7.9 fusion.284
  1104.5 6.3 collective-permute-done.26
  1110.8 9.3 collective-permute-done.25
  1120.1 8.6 collective-permute-done.24
  1131.5 178.1 %all-reduce.18.cloned.1.call-done = (bf16[400,1600]{1,0:T(8,128)(2,1)}, bf16[1600,400]{0,1:T(8,128)(2,1)}, bf16[400,800]{1,0:T(8,128)(2,1)}, bf16[800,3200]{1,0:...) async-done(((bf16[400,1600]{1,0:T(8,128)(2,1)}, bf16[1600,400]{0,1:T(8,128)(2,1)}, ...) | async-done | bytes 16960016 | tf_op jit(solution)/shard_map/psum | solution.py:315
  1331.3 116.5 %all-reduce.14.cloned.1.call-done = (f32[7,7,400]{2,1,0:T(8,128)}, f32[7,7,800]{2,1,0:T(8,128)}, f32[7,7,400]{2,1,0:T(8,128)}) async-done(((f32[7,7,400]{2,1,0:T(8,128)}, f32[7,7,800]{2,1,0:T(8,128)}, f32[7,7,400]{2,1,0:T(8,128)}), (f32[7,7,400]{2,1,0:T(8,128)}, f32[7,7,800]{2,1,0:T(8,128)}, f32[7,7,400]{2,1,0:T(8,128)})) %all-reduce.14.cloned.1.call-update) | async-done | bytes 313616 | tf_op jit(solution)/shard_map/psum | solution.py:338
  (1153 shorter events, 311.1 us)
Async XLA Ops:
  7.2 146.9 %all-gather.19.cloned.1.call-start = ((), (), s32[]{:S(2)}) async-start(), calls=%async_computation.10 | async-start | bytes 1730560 | tf_op jit(solution)/shard_map/all_gather | solution.py:209
  8.0 178.4 %all-gather.11.cloned.1.call-start = ((), (), s32[]{:S(2)}) async-start(), calls=%async_computation.6 | async-start | bytes 2048000 | tf_op jit(solution)/shard_map/all_gather | solution.py:209
  8.7 243.6 %all-gather.13.cloned.1.call-start = ((), (), s32[]{:S(2)}) async-start(), calls=%async_computation.7 | async-start | bytes 6400000 | tf_op jit(solution)/shard_map/all_gather | solution.py:209
  9.5 259.5 %all-gather.15.cloned.1.call-start = ((), (), s32[]{:S(2)}) async-start(), calls=%async_computation.8 | async-start | bytes 7168000 | tf_op jit(solution)/shard_map/all_gather | solution.py:209
  10.1 335.2 %all-gather.21.cloned.1.call-start = ((), (), s32[]{:S(2)}) async-start(), calls=%async_computation.11 | async-start | bytes 1730560 | tf_op jit(solution)/shard_map/all_gather | solution.py:209
  10.6 374.4 %all-gather.17.cloned.1.call-start = ((), (), s32[]{:S(2)}) async-start(), calls=%async_computation.9 | async-start | bytes 2048000 | tf_op jit(solution)/shard_map/all_gather | solution.py:209
  10.8 61.5 %collective-permute-start.2 = (s32[12,32]{1,0:T(8,128)S(1)}, s32[12,32]{1,0:T(8,128)S(1)}, u32[]{:S(2)}, u32[]{:S(2)}) collective-permute-start(s32[12,32]{1,0:T(8,128)S(1)} %bitcast.837), channel_id=1, source_target_pairs={{0,24},{8,16},{16,8},{24,0},{1,25},{9,17},{17,9},{25,1},{2,26},{10... | collective-permute-start | bytes 4616 | tf_op jit(solution)/shard_map/ppermute | solution.py:23
  13.3 67.7 %collective-permute-start.1 = (s32[12,32]{1,0:T(8,128)S(1)}, s32[12,32]{1,0:T(8,128)}, u32[]{:S(2)}, u32[]{:S(2)}) collective-permute-start(s32[12,32]{1,0:T(8,128)S(1)} %bitcast.836), channel_id=1, source_target_pairs={{0,16},{8,24},{16,0},{24,8},{1,17},{9,25},{17,1},{25,9},{2,18},{10... | collective-permute-start | bytes 4616 | tf_op jit(solution)/shard_map/ppermute | solution.py:23
  15.0 69.7 %collective-permute-start.5 = (bf16[12,32,400]{2,1,0:T(8,128)(2,1)}, bf16[12,32,400]{2,1,0:T(8,128)(2,1)}, u32[]{:S(2)}, u32[]{:S(2)}) collective-permute-start(bf16[12,32,400]{2,1,0:T(8,128)(2,1)} %get-tuple-element.379), channel_id=1, source_target_pairs={{0,24},{8,16},{16,8},{24,0},{1,25},{9,17},{17,9},{25,1},{2,26},{10... | collective-permute-start | bytes 921608 | tf_op jit(solution)/shard_map/ppermute | solution.py:23
  16.5 68.9 %collective-permute-start.4 = (bf16[12,32,400]{2,1,0:T(8,128)(2,1)}, bf16[12,32,400]{2,1,0:T(8,128)(2,1)}, u32[]{:S(2)}, u32[]{:S(2)}) collective-permute-start(bf16[12,32,400]{2,1,0:T(8,128)(2,1)} %get-tuple-element.380), channel_id=1, source_target_pairs={{0,16},{8,24},{16,0},{24,8},{1,17},{9,25},{17,1},{25,9},{2,18},{10... | collective-permute-start | bytes 921608 | tf_op jit(solution)/shard_map/ppermute | solution.py:23
  17.0 68.4 %collective-permute-start.3 = (bf16[12,32,400]{2,1,0:T(8,128)(2,1)}, bf16[12,32,400]{2,1,0:T(8,128)(2,1)}, u32[]{:S(2)}, u32[]{:S(2)}) collective-permute-start(bf16[12,32,400]{2,1,0:T(8,128)(2,1)} %get-tuple-element.378), channel_id=1, source_target_pairs={{0,8},{8,0},{16,24},{24,16},{1,9},{9,1},{17,25},{25,17},{2,10},{10... | collective-permute-start | bytes 921608 | tf_op jit(solution)/shard_map/ppermute | solution.py:23
  22.6 117.8 %copy-start.91 = (bf16[7,7,400]{2,1,0:T(8,128)(2,1)}, bf16[7,7,400]{2,1,0:T(8,128)(2,1)S(1)}, u32[]{:S(2)}) copy-start(bf16[7,7,400]{2,1,0:T(8,128)(2,1)S(1)} %rev.9) | copy-start | bytes 117604
  25.6 50.9 %copy-start.372 = (bf16[800]{0:T(1024)(128)(2,1)S(1)}, bf16[800]{0:T(1024)(128)(2,1)}, u32[]{:S(2)}) copy-start(bf16[800]{0:T(1024)(128)(2,1)} %param.41) | copy-start | bytes 4804
  25.6 50.9 %copy-start.391 = (bf16[800]{0:T(1024)(128)(2,1)S(1)}, bf16[800]{0:T(1024)(128)(2,1)}, u32[]{:S(2)}) copy-start(bf16[800]{0:T(1024)(128)(2,1)} %param.46) | copy-start | bytes 4804
  72.3 9.6 collective-permute-start
  74.7 76.9 %copy-start.128 = (f32[400]{0:T(512)}, f32[400]{0:T(512)S(1)}, u32[]{:S(2)}) copy-start(f32[400]{0:T(512)S(1)} %convert_element_type.1430) | copy-start | bytes 4804
  76.5 175.5 %copy-start.121 = (f32[800]{0:T(1024)}, f32[800]{0:T(1024)S(1)}, u32[]{:S(2)}) copy-start(f32[800]{0:T(1024)S(1)} %convert_element_type.1498) | copy-start | bytes 9604
  81.0 159.1 %collective-permute-start.17 = (bf16[12,32,400]{2,1,0:T(8,128)(2,1)}, bf16[12,32,400]{2,1,0:T(8,128)(2,1)}, u32[]{:S(2)}, u32[]{:S(2)}) collective-permute-start(bf16[12,32,400]{2,1,0:T(8,128)(2,1)} %get-tuple-element.387), channel_id=1, source_target_pairs={{0,24},{8,16},{16,8},{24,0},{1,25},{9,17},{17,9},{25,1},{2,26},{10... | collective-permute-start | bytes 921608 | tf_op jit(solution)/shard_map/ppermute | solution.py:23
  81.9 158.3 %collective-permute-start.16 = (bf16[12,32,400]{2,1,0:T(8,128)(2,1)}, bf16[12,32,400]{2,1,0:T(8,128)(2,1)}, u32[]{:S(2)}, u32[]{:S(2)}) collective-permute-start(bf16[12,32,400]{2,1,0:T(8,128)(2,1)} %get-tuple-element.388), channel_id=1, source_target_pairs={{0,16},{8,24},{16,0},{24,8},{1,17},{9,25},{17,1},{25,9},{2,18},{10... | collective-permute-start | bytes 921608 | tf_op jit(solution)/shard_map/ppermute | solution.py:23
  84.7 155.4 %collective-permute-start.15 = (bf16[12,32,400]{2,1,0:T(8,128)(2,1)}, bf16[12,32,400]{2,1,0:T(8,128)(2,1)}, u32[]{:S(2)}, u32[]{:S(2)}) collective-permute-start(bf16[12,32,400]{2,1,0:T(8,128)(2,1)} %get-tuple-element.386), channel_id=1, source_target_pairs={{0,8},{8,0},{16,24},{24,16},{1,9},{9,1},{17,25},{25,17},{2,10},{10... | collective-permute-start | bytes 921608 | tf_op jit(solution)/shard_map/ppermute | solution.py:23
  89.4 3.8 collective-permute-start.7
  89.5 6.9 collective-permute-start.6
  132.3 18.1 %all-to-all-start = ((f32[32,3,400]{2,1,0:T(4,128)}), f32[32,3,400]{2,1,0:T(4,128)S(1)}, u32[]{:S(2)}, u32[]{:S(2)}) async-start(f32[32,3,400]{2,1,0:T(4,128)} %broadcast_in_dim.12), calls=%async_computation | async-start | bytes 524288 | tf_op jit(solution)/shard_map/all_to_all | solution.py:75
  141.7 61.3 %copy-start.100 = (f32[24,2,16,2]{2,3,1,0:T(2,128)}, f32[24,2,16,2]{2,3,1,0:T(2,128)S(1)}, u32[]{:S(2)}) copy-start(f32[24,2,16,2]{2,3,1,0:T(2,128)S(1)} %copy.198) | copy-start | bytes 18436
  210.6 4.0 collective-permute-start.9
  210.6 5.3 collective-permute-start.8
  229.9 20.8 %all-to-all-start.1 = ((f32[32,3,800]{2,1,0:T(4,128)}), f32[32,3,800]{2,1,0:T(4,128)S(1)}, u32[]{:S(2)}, u32[]{:S(2)}) async-start(f32[32,3,800]{2,1,0:T(4,128)} %broadcast_in_dim.13), calls=%async_computation.1 | async-start | bytes 917504 | tf_op jit(solution)/shard_map/all_to_all | solution.py:75
  291.4 5.5 collective-permute-start.11
  294.1 5.9 collective-permute-start.10
  333.9 15.2 %all-to-all-start.2 = ((f32[32,3,400]{2,1,0:T(4,128)}), f32[32,3,400]{2,1,0:T(4,128)}, u32[]{:S(2)}, u32[]{:S(2)}) async-start(f32[32,3,400]{2,1,0:T(4,128)} %broadcast_in_dim.14), calls=%async_computation.2 | async-start | bytes 524288 | tf_op jit(solution)/shard_map/all_to_all | solution.py:75
  407.5 14.7 %all-to-all-start.3 = ((f32[32,2,400]{2,1,0:T(2,128)}), f32[32,2,400]{2,1,0:T(2,128)}, u32[]{:S(2)}, u32[]{:S(2)}) async-start(f32[32,2,400]{2,1,0:T(2,128)} %broadcast_in_dim.15), calls=%async_computation.3 | async-start | bytes 262144 | tf_op jit(solution)/shard_map/all_to_all | solution.py:75
  434.9 7.6 collective-permute-start.19
  435.0 7.5 collective-permute-start.18
  514.3 20.0 %all-to-all-start.4 = ((f32[32,2,800]{2,1,0:T(2,128)}), f32[32,2,800]{2,1,0:T(2,128)}, u32[]{:S(2)}, u32[]{:S(2)}) async-start(f32[32,2,800]{2,1,0:T(2,128)} %broadcast_in_dim.16), calls=%async_computation.4 | async-start | bytes 458752 | tf_op jit(solution)/shard_map/all_to_all | solution.py:75
  523.0 439.0 %all-reduce.16.cloned.1.call-start = ((), (), s32[]{:S(2)}) async-start(), calls=%async_computation.13 | async-start | bytes 34611200 | tf_op jit(solution)/shard_map/psum | solution.py:315
  544.0 8.3 collective-permute-start.21
  544.1 8.2 collective-permute-start.20
  609.3 700.4 %all-reduce.18.cloned.1.call-start = ((), (), s32[]{:S(2)}) async-start(), calls=%async_computation.14 | async-start | bytes 34611200 | tf_op jit(solution)/shard_map/psum | solution.py:315
  638.8 323.2 %collective-permute-start.14 = (bf16[12,32,400]{2,1,0:T(8,128)(2,1)}, bf16[12,32,400]{2,1,0:T(8,128)(2,1)}, u32[]{:S(2)}, u32[]{:S(2)}) collective-permute-start(bf16[12,32,400]{2,1,0:T(8,128)(2,1)} %get-tuple-element.362), channel_id=1, source_target_pairs={{0,24},{8,16},{16,8},{24,0},{1,25},{9,17},{17,9},{25,1},{2,26},{10... | collective-permute-start | bytes 921608 | tf_op jit(solution)/shard_map/ppermute | solution.py:43
  641.1 320.9 %collective-permute-start.13 = (bf16[12,32,400]{2,1,0:T(8,128)(2,1)}, bf16[12,32,400]{2,1,0:T(8,128)(2,1)}, u32[]{:S(2)}, u32[]{:S(2)}) collective-permute-start(bf16[12,32,400]{2,1,0:T(8,128)(2,1)} %get-tuple-element.363), channel_id=1, source_target_pairs={{0,16},{8,24},{16,0},{24,8},{1,17},{9,25},{17,1},{25,9},{2,18},{10... | collective-permute-start | bytes 921608 | tf_op jit(solution)/shard_map/ppermute | solution.py:43
  641.7 320.3 %collective-permute-start.12 = (bf16[12,32,400]{2,1,0:T(8,128)(2,1)}, bf16[12,32,400]{2,1,0:T(8,128)(2,1)}, u32[]{:S(2)}, u32[]{:S(2)}) collective-permute-start(bf16[12,32,400]{2,1,0:T(8,128)(2,1)} %get-tuple-element.364), channel_id=1, source_target_pairs={{0,8},{8,0},{16,24},{24,16},{1,9},{9,1},{17,25},{25,17},{2,10},{10... | collective-permute-start | bytes 921608 | tf_op jit(solution)/shard_map/ppermute | solution.py:43
  984.2 55.8 %all-to-all-start.5 = ((f32[32,2,400]{2,1,0:T(2,128)}), f32[32,2,400]{2,1,0:T(2,128)}, u32[]{:S(2)}, u32[]{:S(2)}) async-start(f32[32,2,400]{2,1,0:T(2,128)} %broadcast_in_dim.17), calls=%async_computation.5 | async-start | bytes 262144 | tf_op jit(solution)/shard_map/all_to_all | solution.py:75
  989.3 458.6 %all-reduce.14.cloned.1.call-start = ((), (), s32[]{:S(2)}) async-start(), calls=%async_computation.12 | async-start | bytes 860160 | tf_op jit(solution)/shard_map/psum | solution.py:338
  1051.9 10.7 collective-permute-start.23
  1052.2 10.4 collective-permute-start.22
  1089.4 21.4 %collective-permute-start.26 = (bf16[12,32,400]{2,1,0:T(8,128)(2,1)}, bf16[12,32,400]{2,1,0:T(8,128)(2,1)S(1)}, u32[]{:S(2)}, u32[]{:S(2)}) collective-permute-start(bf16[12,32,400]{2,1,0:T(8,128)(2,1)} %get-tuple-element.350), channel_id=1, source_target_pairs={{0,24},{8,16},{16,8},{24,0},{1,25},{9,17},{17,9},{25,1},{2,26},{10... | collective-permute-start | bytes 921608 | tf_op jit(solution)/shard_map/ppermute | solution.py:43
  1091.8 28.3 %collective-permute-start.25 = (bf16[12,32,400]{2,1,0:T(8,128)(2,1)}, bf16[12,32,400]{2,1,0:T(8,128)(2,1)S(1)}, u32[]{:S(2)}, u32[]{:S(2)}) collective-permute-start(bf16[12,32,400]{2,1,0:T(8,128)(2,1)} %get-tuple-element.351), channel_id=1, source_target_pairs={{0,16},{8,24},{16,0},{24,8},{1,17},{9,25},{17,1},{25,9},{2,18},{10... | collective-permute-start | bytes 921608 | tf_op jit(solution)/shard_map/ppermute | solution.py:43
  1093.3 35.4 %collective-permute-start.24 = (bf16[12,32,400]{2,1,0:T(8,128)(2,1)}, bf16[12,32,400]{2,1,0:T(8,128)(2,1)}, u32[]{:S(2)}, u32[]{:S(2)}) collective-permute-start(bf16[12,32,400]{2,1,0:T(8,128)(2,1)} %get-tuple-element.352), channel_id=1, source_target_pairs={{0,8},{8,0},{16,24},{24,16},{1,9},{9,1},{17,25},{25,17},{2,10},{10... | collective-permute-start | bytes 921608 | tf_op jit(solution)/shard_map/ppermute | solution.py:43
  (402 other events, 3294.5 us)
Sparse Core Ops, SparseCore 0:
  9.9 45.7 all-gather.18
  57.6 47.5 all-gather.10
  107.0 63.3 all-gather.12
  172.1 65.5 all-gather.14
  239.3 29.5 all-gather.20
  270.6 31.5 all-gather.16
  609.4 352.5 all-reduce.15
  967.3 342.2 all-reduce.17
  1318.1 129.6 all-reduce.13
